TPU v7x, 128 devices: a whole 4x4x4 slice. The times are simulated.
128 devices in a mesh: dom: 32 (over y, x, core), near: 4 (over z).
Axes of the slice: x: 4, y: 4, z: 4, core: 2. Of those that a mesh axis runs over, the one named last changes fastest.
Arguments:
- start_block: float32 [131072, 128], P(('dom', 'near')), may hold values from -6 to 6
- near_tiles: float32 [6144, 128, 128], P(('dom', 'near')), may hold values from -0.09375 to 0.09375
- near_src: int32 [6144], P(('dom', 'near')), may hold values from 0 to 31, as said below
- near_mask: int32 [6144], P(('dom', 'near')), may hold values 0 or 1
- far_tiles: float32 [1024, 128, 128], P(('dom', 'near')), may hold values from -0.09375 to 0.09375
- far_src: int32 [1024], P(('dom', 'near')), may hold values from 0 to 31
- far_mask: int32 [1024], P(('dom', 'near')), may hold values 0 or 1
- bound_count: int32 [128], P(('dom', 'near')), may hold values from 1 to 128
Outputs:
- encodings: float32 [131072, 128], P(('dom', 'near'))
- rayleigh: float32 [128, 128], replicated
Inputs may be any that keep to these rules, and one draw needn't show every extreme that they name: `near_src`: each partition holds 48 consecutive slots; the slot at position j among them (j from 0) lies in tile row j // 6; the first slot of each tile row reads the partition's own tile of that row; every source tile from another partition of the group is one of that partition's first 4 tiles.
All inputs are finite; a program needn't handle non-finite values. No bound on the sum of `near_mask` or of `far_mask` on one device may be relied on, other than what follows from the above.
Results may differ from a plain program's by a relative error of at most 0.0003.
Values sent between devices are 32-bit elements; how exact they have to be, the bound alone decides.
No kernel may reach another device: no remote copies, remote signals or barrier semaphores. Data moves between devices by JAX's collectives and lax.ppermute only.
A program may use at most 64 MiB of HBM per device.

v0:
```python
from functools import partial
import jax
import jax.numpy as jnp
from jax import lax
from jax.sharding import PartitionSpec as P

NPER = 6
ITERS = 2
DEG = 3
LOWER_EDGE = 0.6
UPPER_EDGE = 2.0


def apply_operator(
    block, near_tiles, near_src, near_mask, far_tiles, far_src, far_mask, bound_count
):
    tile_rows = near_tiles.shape[1]
    width = block.shape[1]
    tiles_dev = block.shape[0] // tile_rows
    group_size = lax.axis_size("near")
    gathered = lax.all_gather(block, "near", axis=0, tiled=True)
    picked = gathered.reshape(group_size * tiles_dev, tile_rows, width)[near_src]
    products = jnp.einsum("sij,sjk->sik", near_tiles, picked, precision=lax.Precision.HIGHEST)
    products = products * near_mask.astype(jnp.float32)[:, None, None]
    near_sum = products.reshape(tiles_dev, NPER, tile_rows, width).sum(axis=1)
    limit = (jnp.arange(tile_rows) < bound_count[0]).astype(jnp.float32)
    edge_tile = block[:tile_rows] * limit[:, None]
    edges = lax.all_gather(edge_tile, "dom", axis=0, tiled=True).reshape(
        lax.axis_size("dom"), tile_rows, width
    )
    far_pick = edges[far_src]
    far_sum = jnp.einsum("sij,sjk->sik", far_tiles, far_pick, precision=lax.Precision.HIGHEST)
    far_sum = far_sum * far_mask.astype(jnp.float32)[:, None, None]
    return block - (near_sum + far_sum).reshape(block.shape)


def chebyshev(current, image, operator):
    center = (UPPER_EDGE + LOWER_EDGE) / 2.0
    half = (UPPER_EDGE - LOWER_EDGE) / 2.0
    previous = current
    present = (image - center * current) / half
    for degree in range(DEG - 1):
        following = 2.0 * (operator(present) - center * present) / half - previous
        previous, present = (present, following)
    return present


def inner(left, right):
    return jnp.dot(
        left.T, right, precision=lax.Precision.HIGHEST, preferred_element_type=jnp.float32
    )


def times_inverse(block, lower_inv):
    return jnp.dot(
        block, lower_inv.T, precision=lax.Precision.HIGHEST, preferred_element_type=jnp.float32
    )


def inverse_factor(gram):
    lower = jnp.linalg.cholesky(gram)
    return jax.scipy.linalg.solve_triangular(
        lower, jnp.eye(gram.shape[0], dtype=jnp.float32), lower=True
    )


def local(start_block, near_tiles, near_src, near_mask, far_tiles, far_src, far_mask, bound_count):
    operator = partial(
        apply_operator,
        near_tiles=near_tiles,
        near_src=near_src,
        near_mask=near_mask,
        far_tiles=far_tiles,
        far_src=far_src,
        far_mask=far_mask,
        bound_count=bound_count,
    )
    nodes_all = start_block.shape[0] * lax.axis_size("dom") * lax.axis_size("near")
    current = start_block
    image = operator(current)
    for iteration in range(ITERS):
        if iteration > 0:
            image = operator(current)
        filtered = chebyshev(current, image, operator)
        gram = lax.psum(inner(filtered, filtered), ("dom", "near")) / nodes_all
        lower_inv = inverse_factor(gram)
        current = times_inverse(filtered, lower_inv)
    final_image = operator(current)
    rayleigh = lax.psum(inner(current, final_image), ("dom", "near")) / nodes_all
    return (current, rayleigh)


def solution(mesh):
    return jax.shard_map(
        local,
        mesh=mesh,
        in_specs=(
            P(("dom", "near"), None),
            P(("dom", "near"), None, None),
            P(("dom", "near")),
            P(("dom", "near")),
            P(("dom", "near"), None, None),
            P(("dom", "near")),
            P(("dom", "near")),
            P(("dom", "near")),
        ),
        out_specs=(P(("dom", "near"), None), P()),
        check_vma=False,
    )
```

profile of v0, /device:TPU:1, one launch (start us, length us, event | category | flops | bytes accessed | tf_op | source)
XLA Modules:
  0.0 1082.7 jit_solution(1137057290617790462)
XLA Ops:
  13.1 30.7 %all-gather.15.cloned.1.call-done = f32[4096,128]{1,0:T(8,128)} async-done(((f32[1024,128]{1,0:T(8,128)}), f32[4096,128]{1,0:T(8,128)}) %all-gather.15.cloned.1.call-update) | async-done | bytes 2097168 | tf_op jit(solution)/shard_map/all_gather | solution.py:21
  47.7 8.1 convolution_multiply_fusion.6
  60.8 29.6 %all-gather.17.cloned.1.call-done = f32[4096,128]{1,0:T(8,128)} async-done(((f32[128,128]{1,0:T(8,128)}), f32[4096,128]{1,0:T(8,128)}) %all-gather.17.cloned.1.call-update) | async-done | bytes 2097168 | tf_op jit(solution)/shard_map/all_gather | solution.py:28
  99.8 28.3 %all-gather.19.cloned.1.call-done = f32[4096,128]{1,0:T(8,128)} async-done(((f32[1024,128]{1,0:T(8,128)}), f32[4096,128]{1,0:T(8,128)}) %all-gather.19.cloned.1.call-update) | async-done | bytes 2097168 | tf_op jit(solution)/shard_map/all_gather | solution.py:21
  145.2 29.5 %all-gather.21.cloned.1.call-done = f32[4096,128]{1,0:T(8,128)} async-done(((f32[128,128]{1,0:T(8,128)}), f32[4096,128]{1,0:T(8,128)}) %all-gather.21.cloned.1.call-update) | async-done | bytes 2097168 | tf_op jit(solution)/shard_map/all_gather | solution.py:28
  184.5 28.1 %all-gather.23.cloned.1.call-done = f32[4096,128]{1,0:T(8,128)} async-done(((f32[1024,128]{1,0:T(8,128)}), f32[4096,128]{1,0:T(8,128)}) %all-gather.23.cloned.1.call-update) | async-done | bytes 2097168 | tf_op jit(solution)/shard_map/all_gather | solution.py:21
  216.5 8.1 convolution_multiply_fusion.4
  229.7 29.5 %all-gather.25.cloned.1.call-done = f32[4096,128]{1,0:T(8,128)} async-done(((f32[128,128]{1,0:T(8,128)}), f32[4096,128]{1,0:T(8,128)}) %all-gather.25.cloned.1.call-update) | async-done | bytes 2097168 | tf_op jit(solution)/shard_map/all_gather | solution.py:28
  268.2 138.8 %all-reduce.4.cloned.1.call-done = f32[128,128]{0,1:T(8,128)} async-done(((f32[128,128]{0,1:T(8,128)}), f32[128,128]{0,1:T(8,128)}) %all-reduce.4.cloned.1.call-update) | async-done | bytes 65552 | tf_op jit(solution)/shard_map/psum | solution.py:85
  408.8 11.7 %cholesky.44 = f32[128,128]{1,0:T(8,128)S(1)} custom-call(f32[128,128]{1,0:T(8,128)S(1)} %fusion.41), custom_call_target="Cholesky" | custom-call | tf_op jit(solution)/shard_map/jit(cholesky)/cholesky | solution.py:61
  421.9 9.8 custom-call.6
  436.1 26.2 %all-gather.27.cloned.1.call-done = f32[4096,128]{1,0:T(8,128)} async-done(((f32[1024,128]{1,0:T(8,128)}), f32[4096,128]{1,0:T(8,128)}) %all-gather.27.cloned.1.call-update) | async-done | bytes 2097168 | tf_op jit(solution)/shard_map/all_gather | solution.py:21
  466.3 8.1 convolution_multiply_fusion.3
  479.4 29.6 %all-gather.29.cloned.1.call-done = f32[4096,128]{1,0:T(8,128)} async-done(((f32[128,128]{1,0:T(8,128)}), f32[4096,128]{1,0:T(8,128)}) %all-gather.29.cloned.1.call-update) | async-done | bytes 2097168 | tf_op jit(solution)/shard_map/all_gather | solution.py:28
  518.6 28.1 %all-gather.31.cloned.1.call-done = f32[4096,128]{1,0:T(8,128)} async-done(((f32[1024,128]{1,0:T(8,128)}), f32[4096,128]{1,0:T(8,128)}) %all-gather.31.cloned.1.call-update) | async-done | bytes 2097168 | tf_op jit(solution)/shard_map/all_gather | solution.py:21
  563.8 29.6 %all-gather.33.cloned.1.call-done = f32[4096,128]{1,0:T(8,128)} async-done(((f32[128,128]{1,0:T(8,128)}), f32[4096,128]{1,0:T(8,128)}) %all-gather.33.cloned.1.call-update) | async-done | bytes 2097168 | tf_op jit(solution)/shard_map/all_gather | solution.py:28
  603.0 28.3 %all-gather.35.cloned.1.call-done = f32[4096,128]{1,0:T(8,128)} async-done(((f32[1024,128]{1,0:T(8,128)}), f32[4096,128]{1,0:T(8,128)}) %all-gather.35.cloned.1.call-update) | async-done | bytes 2097168 | tf_op jit(solution)/shard_map/all_gather | solution.py:21
  648.4 29.6 %all-gather.37.cloned.1.call-done = f32[4096,128]{1,0:T(8,128)} async-done(((f32[128,128]{1,0:T(8,128)}), f32[4096,128]{1,0:T(8,128)}) %all-gather.37.cloned.1.call-update) | async-done | bytes 2097168 | tf_op jit(solution)/shard_map/all_gather | solution.py:28
  687.5 138.4 %all-reduce.6.cloned.1.call-done = f32[128,128]{0,1:T(8,128)} async-done(((f32[128,128]{0,1:T(8,128)}), f32[128,128]{0,1:T(8,128)}) %all-reduce.6.cloned.1.call-update) | async-done | bytes 65552 | tf_op jit(solution)/shard_map/psum | solution.py:85
  827.7 11.7 %cholesky.55 = f32[128,128]{1,0:T(8,128)S(1)} custom-call(f32[128,128]{1,0:T(8,128)S(1)} %fusion.39), custom_call_target="Cholesky" | custom-call | tf_op jit(solution)/shard_map/jit(cholesky)/cholesky | solution.py:61
  840.8 9.8 custom-call.7
  855.2 26.0 %all-gather.39.cloned.1.call-done = f32[4096,128]{1,0:T(8,128)} async-done(((f32[1024,128]{1,0:T(8,128)}), f32[4096,128]{1,0:T(8,128)}) %all-gather.39.cloned.1.call-update) | async-done | bytes 2097168 | tf_op jit(solution)/shard_map/all_gather | solution.py:21
  898.3 29.5 %all-gather.41.cloned.1.call-done = f32[4096,128]{1,0:T(8,128)} async-done(((f32[128,128]{1,0:T(8,128)}), f32[4096,128]{1,0:T(8,128)}) %all-gather.41.cloned.1.call-update) | async-done | bytes 2097168 | tf_op jit(solution)/shard_map/all_gather | solution.py:28
  935.5 138.9 %all-reduce.8.cloned.1.call-done = f32[128,128]{0,1:T(8,128)} async-done(((f32[128,128]{0,1:T(8,128)}), f32[128,128]{0,1:T(8,128)}) %all-reduce.8.cloned.1.call-update) | async-done | bytes 65552 | tf_op jit(solution)/shard_map/psum | solution.py:89
  (128 shorter events, 181.6 us)
Async XLA Ops:
  7.2 40.5 %copy-start = (f32[48,128,128]{2,1,0:T(8,128)S(1)}, f32[48,128,128]{2,1,0:T(8,128)}, u32[]{:S(2)}) copy-start(f32[48,128,128]{2,1,0:T(8,128)} %param.12) | copy-start | bytes 9437188
  7.2 36.5 %all-gather.15.cloned.1.call-start = ((), (), s32[]{:S(2)}) async-start(), calls=%async_computation | async-start | bytes 2621440 | tf_op jit(solution)/shard_map/all_gather | solution.py:21
  7.9 82.5 %all-gather.17.cloned.1.call-start = ((), (), s32[]{:S(2)}) async-start(), calls=%async_computation.1 | async-start | bytes 2162688 | tf_op jit(solution)/shard_map/all_gather | solution.py:28
  10.4 117.7 %all-gather.19.cloned.1.call-start = ((), (), s32[]{:S(2)}) async-start(), calls=%async_computation.2 | async-start | bytes 2621440 | tf_op jit(solution)/shard_map/all_gather | solution.py:21
  95.4 0.8 copy-start.2
  98.1 76.5 %all-gather.21.cloned.1.call-start = ((), (), s32[]{:S(2)}) async-start(), calls=%async_computation.3 | async-start | bytes 2162688 | tf_op jit(solution)/shard_map/all_gather | solution.py:28
  99.8 112.8 %all-gather.23.cloned.1.call-start = ((), (), s32[]{:S(2)}) async-start(), calls=%async_computation.4 | async-start | bytes 2621440 | tf_op jit(solution)/shard_map/all_gather | solution.py:21
  179.6 0.8 copy-start.6
  182.6 76.5 %all-gather.25.cloned.1.call-start = ((), (), s32[]{:S(2)}) async-start(), calls=%async_computation.5 | async-start | bytes 2162688 | tf_op jit(solution)/shard_map/all_gather | solution.py:28
  184.2 222.8 %all-reduce.4.cloned.1.call-start = ((), (), s32[]{:S(2)}) async-start(), calls=%async_computation.6 | async-start | bytes 131072 | tf_op jit(solution)/shard_map/psum | solution.py:85
  265.7 0.8 copy-start.4
  268.1 194.2 %all-gather.27.cloned.1.call-start = ((), (), s32[]{:S(2)}) async-start(), calls=%async_computation.7 | async-start | bytes 2621440 | tf_op jit(solution)/shard_map/all_gather | solution.py:21
  434.5 74.6 %all-gather.29.cloned.1.call-start = ((), (), s32[]{:S(2)}) async-start(), calls=%async_computation.8 | async-start | bytes 2162688 | tf_op jit(solution)/shard_map/all_gather | solution.py:28
  436.1 110.6 %all-gather.31.cloned.1.call-start = ((), (), s32[]{:S(2)}) async-start(), calls=%async_computation.9 | async-start | bytes 2621440 | tf_op jit(solution)/shard_map/all_gather | solution.py:21
  514.0 0.8 copy-start.1
  516.7 76.7 %all-gather.33.cloned.1.call-start = ((), (), s32[]{:S(2)}) async-start(), calls=%async_computation.10 | async-start | bytes 2162688 | tf_op jit(solution)/shard_map/all_gather | solution.py:28
  518.4 112.9 %all-gather.35.cloned.1.call-start = ((), (), s32[]{:S(2)}) async-start(), calls=%async_computation.11 | async-start | bytes 2621440 | tf_op jit(solution)/shard_map/all_gather | solution.py:21
  598.3 0.8 copy-start.5
  601.3 76.7 %all-gather.37.cloned.1.call-start = ((), (), s32[]{:S(2)}) async-start(), calls=%async_computation.12 | async-start | bytes 2162688 | tf_op jit(solution)/shard_map/all_gather | solution.py:28
  603.0 223.0 %all-reduce.6.cloned.1.call-start = ((), (), s32[]{:S(2)}) async-start(), calls=%async_computation.13 | async-start | bytes 131072 | tf_op jit(solution)/shard_map/psum | solution.py:85
  684.6 0.8 copy-start.3
  687.0 194.1 %all-gather.39.cloned.1.call-start = ((), (), s32[]{:S(2)}) async-start(), calls=%async_computation.14 | async-start | bytes 2621440 | tf_op jit(solution)/shard_map/all_gather | solution.py:21
  853.3 74.4 %all-gather.41.cloned.1.call-start = ((), (), s32[]{:S(2)}) async-start(), calls=%async_computation.15 | async-start | bytes 2162688 | tf_op jit(solution)/shard_map/all_gather | solution.py:28
  855.0 219.5 %all-reduce.8.cloned.1.call-start = ((), (), s32[]{:S(2)}) async-start(), calls=%async_computation.16 | async-start | bytes 131072 | tf_op jit(solution)/shard_map/psum | solution.py:89
Sparse Core Ops, SparseCore 0:
  9.6 34.0 all-gather.14
  46.5 43.8 all-gather.16
  98.3 29.7 all-gather.18
  130.8 43.8 all-gather.20
  182.7 29.7 all-gather.22
  215.2 43.8 all-gather.24
  268.3 138.7 all-reduce.3
  434.6 27.6 all-gather.26
  465.1 43.8 all-gather.28
  516.9 29.7 all-gather.30
  549.5 43.8 all-gather.32
  601.5 29.7 all-gather.34
  634.1 43.8 all-gather.36
  687.1 138.7 all-reduce.5
  853.4 27.6 all-gather.38
  883.9 43.8 all-gather.40
  935.7 138.7 all-reduce.7
where the time goes:
time: 1090 us; the launch traced here: 1080 us
  waiting for transfers between devices  819 us (75%)
  other arithmetic  95.5 us (9%)
  matrix products  82.2 us (8%)
  local copies, waits for them, and re-layouts  68.7 us (6%)
  between operations  15.2 us (1%)
    psum x2, waiting for transfers between devices, local(): gram = lax.psum(inner(filtered, filtered), ('dom', 'near')) / nodes_all  277 us
    all_gather x7, waiting for transfers between devices, apply_operator(): lax.all_gather(edge_tile, 'dom', axis=0, tiled=True)  207 us
    all_gather x7, waiting for transfers between devices, apply_operator(): gathered = lax.all_gather(block, 'near', axis=0, tiled=True)  196 us
    psum x1, waiting for transfers between devices, local(): lax.psum(inner(current, final_image), ('dom', 'near')) / nodes_all  139 us
    dot_general x7, matrix products, apply_operator(): jnp.einsum('sij,sjk->sik', near_tiles, picked, precision=lax.Precision.HI...  56.9 us
    gather x7, local copies, waits for them, and re-layouts, apply_operator(): gathered.reshape(group_size * tiles_dev, tile_rows, width)[near_src]  28 us
    another operation x6, other arithmetic, inverse_factor(): lower = jnp.linalg.cholesky(gram)  24.8 us
  transfers between devices with their start and end apart: 17, of which 17 were waited for; matrix products, arithmetic and copies ran while one was open for 12% of the time, Pallas kernels for 0%

commit v1 on v0

--- a/solution.py
+++ b/solution.py
@@ -18,7 +18,12 @@
     width = block.shape[1]
     tiles_dev = block.shape[0] // tile_rows
     group_size = lax.axis_size("near")
-    gathered = lax.all_gather(block, "near", axis=0, tiled=True)
+    ring = [block]
+    for hop in range(3):
+        ring.append(lax.ppermute(ring[-1], "near", [(dev, (dev + 1) % 4) for dev in range(4)]))
+    gathered = jnp.roll(
+        jnp.concatenate(ring[::-1], axis=0), (lax.axis_index("near") + 1) * ring[0].shape[0], axis=0
+    )
     picked = gathered.reshape(group_size * tiles_dev, tile_rows, width)[near_src]
     products = jnp.einsum("sij,sjk->sik", near_tiles, picked, precision=lax.Precision.HIGHEST)
     products = products * near_mask.astype(jnp.float32)[:, None, None]

time: 1090 us -> 1000 us (0.917)
  waiting for transfers between devices: 819 us -> 680 us
  other arithmetic: 95.5 us -> 132 us
    ppermute x0 -> x21, waiting for transfers between devices: none -> 254 us  [apply_operator(): lax.ppermute(ring[-1], 'near', [(dev, (dev + 1) % 4) for dev in range(4)])]
    all_gather x7, waiting for transfers between devices: 207 us -> 0.01 us  [apply_operator(): lax.all_gather(edge_tile, 'dom', axis=0, tiled=True)]
    all_gather x7 -> x0, waiting for transfers between devices: 196 us -> none  [apply_operator(): gathered = lax.all_gather(block, 'near', axis=0, tiled=True)]
    concatenate x0 -> x7, other arithmetic: none -> 45.2 us  [apply_operator(): jnp.roll(jnp.concatenate(ring[::-1], axis=0), (lax.axis_index('near') + 1...]
    psum x2, waiting for transfers between devices: 277 us -> 289 us  [local(): gram = lax.psum(inner(filtered, filtered), ('dom', 'near')) / nodes_all]
  transfers between devices with their start and end apart: 17 -> 31, of which waited for: 17 -> 24; matrix products, arithmetic and copies ran while one was open for 12% -> 17% of each run, Pallas kernels for 0% -> 0%
where the time goes in v1:
time: 1000 us; the launch traced here: 994 us
  waiting for transfers between devices  680 us (68%)
  other arithmetic  132 us (13%)
  matrix products  80.6 us (8%)
  local copies, waits for them, and re-layouts  74.2 us (7%)
  between operations  15.8 us (2%)
  starting transfers between devices  10.8 us (1%)
    psum x2, waiting for transfers between devices, local(): gram = lax.psum(inner(filtered, filtered), ('dom', 'near')) / nodes_all  289 us
    ppermute x21, waiting for transfers between devices, apply_operator(): lax.ppermute(ring[-1], 'near', [(dev, (dev + 1) % 4) for dev in range(4)])  254 us
    psum x1, waiting for transfers between devices, local(): lax.psum(inner(current, final_image), ('dom', 'near')) / nodes_all  137 us
    dot_general x7, matrix products, apply_operator(): jnp.einsum('sij,sjk->sik', near_tiles, picked, precision=lax.Precision.HI...  56.8 us
    concatenate x7, other arithmetic, apply_operator(): jnp.roll(jnp.concatenate(ring[::-1], axis=0), (lax.axis_index('near') + 1...  45.2 us
    gather x7, local copies, waits for them, and re-layouts, apply_operator(): gathered.reshape(group_size * tiles_dev, tile_rows, width)[near_src]  27.9 us
    another operation x6, other arithmetic, inverse_factor(): lower = jnp.linalg.cholesky(gram)  24.8 us
    another operation x4, other arithmetic, inverse_factor(): jax.scipy.linalg.solve_triangular(lower, jnp.eye(gram.shape[0], dtype=jnp...  20.9 us
  transfers between devices with their start and end apart: 31, of which 24 were waited for; matrix products, arithmetic and copies ran while one was open for 17% of the time, Pallas kernels for 0%

profile of v1, /device:TPU:1, one launch (start us, length us, event | category | flops | bytes accessed | tf_op | source)
XLA Modules:
  0.0 994.0 jit_solution(772266820513304977)
XLA Ops:
  12.3 14.0 %collective-permute-done = f32[1024,128]{1,0:T(8,128)S(1)} collective-permute-done((f32[1024,128]{1,0:T(8,128)}, f32[1024,128]{1,0:T(8,128)S(1)}, u32[]{:S(2)}, u32[]{:S(2)}) %collective-permute-start) | collective-permute-done | bytes 524320 | tf_op jit(solution)/shard_map/ppermute | solution.py:23
  27.0 13.5 %collective-permute-done.1 = f32[1024,128]{1,0:T(8,128)} collective-permute-done((f32[1024,128]{1,0:T(8,128)S(1)}, f32[1024,128]{1,0:T(8,128)}, u32[]{:S(2)}, u32[]{:S(2)}) %collective-permute-start.1) | collective-permute-done | bytes 524320 | tf_op jit(solution)/shard_map/ppermute | solution.py:23
  43.2 10.3 %collective-permute-done.2 = f32[1024,128]{1,0:T(8,128)} collective-permute-done((f32[1024,128]{1,0:T(8,128)}, f32[1024,128]{1,0:T(8,128)}, u32[]{:S(2)}, u32[]{:S(2)}) %collective-permute-start.2) | collective-permute-done | bytes 524320 | tf_op jit(solution)/shard_map/ppermute | solution.py:23
  84.5 11.9 %collective-permute-done.3 = f32[1024,128]{1,0:T(8,128)S(1)} collective-permute-done((f32[1024,128]{1,0:T(8,128)}, f32[1024,128]{1,0:T(8,128)S(1)}, u32[]{:S(2)}, u32[]{:S(2)}) %collective-permute-start.3) | collective-permute-done | bytes 524320 | tf_op jit(solution)/shard_map/ppermute | solution.py:23
  96.4 10.8 %collective-permute-done.4 = f32[1024,128]{1,0:T(8,128)S(1)} collective-permute-done((f32[1024,128]{1,0:T(8,128)S(1)}, f32[1024,128]{1,0:T(8,128)S(1)}, u32[]{:S(2)}, u32[]{:S(2)}) %collective-permute-start.4) | collective-permute-done | bytes 524320 | tf_op jit(solution)/shard_map/ppermute | solution.py:23
  159.5 12.0 %collective-permute-done.7 = f32[1024,128]{1,0:T(8,128)S(1)} collective-permute-done((f32[1024,128]{1,0:T(8,128)S(1)}, f32[1024,128]{1,0:T(8,128)S(1)}, u32[]{:S(2)}, u32[]{:S(2)}) %collective-permute-start.7) | collective-permute-done | bytes 524320 | tf_op jit(solution)/shard_map/ppermute | solution.py:23
  171.8 12.1 %collective-permute-done.8 = f32[1024,128]{1,0:T(8,128)S(1)} collective-permute-done((f32[1024,128]{1,0:T(8,128)S(1)}, f32[1024,128]{1,0:T(8,128)S(1)}, u32[]{:S(2)}, u32[]{:S(2)}) %collective-permute-start.8) | collective-permute-done | bytes 524320 | tf_op jit(solution)/shard_map/ppermute | solution.py:23
  216.9 146.8 %all-reduce.4.cloned.1.call-done = f32[128,128]{0,1:T(8,128)} async-done(((f32[128,128]{0,1:T(8,128)}), f32[128,128]{0,1:T(8,128)}) %all-reduce.4.cloned.1.call-update) | async-done | bytes 65552 | tf_op jit(solution)/shard_map/psum | solution.py:90
  365.5 11.7 %cholesky.44 = f32[128,128]{1,0:T(8,128)S(1)} custom-call(f32[128,128]{1,0:T(8,128)S(1)} %fusion.90), custom_call_target="Cholesky" | custom-call | tf_op jit(solution)/shard_map/jit(cholesky)/cholesky | solution.py:66
  393.1 12.5 %collective-permute-done.9 = f32[1024,128]{1,0:T(8,128)S(1)} collective-permute-done((f32[1024,128]{1,0:T(8,128)}, f32[1024,128]{1,0:T(8,128)S(1)}, u32[]{:S(2)}, u32[]{:S(2)}) %collective-permute-start.9) | collective-permute-done | bytes 524320 | tf_op jit(solution)/shard_map/ppermute | solution.py:23
  407.2 13.5 %collective-permute-done.10 = f32[1024,128]{1,0:T(8,128)S(1)} collective-permute-done((f32[1024,128]{1,0:T(8,128)S(1)}, f32[1024,128]{1,0:T(8,128)S(1)}, u32[]{:S(2)}, u32[]{:S(2)}) %collective-permute-start.10) | collective-permute-done | bytes 524320 | tf_op jit(solution)/shard_map/ppermute | solution.py:23
  420.9 14.2 %collective-permute-done.11 = f32[1024,128]{1,0:T(8,128)S(1)} collective-permute-done((f32[1024,128]{1,0:T(8,128)S(1)}, f32[1024,128]{1,0:T(8,128)S(1)}, u32[]{:S(2)}, u32[]{:S(2)}) %collective-permute-start.11) | collective-permute-done | bytes 524320 | tf_op jit(solution)/shard_map/ppermute | solution.py:23
  467.3 13.5 %collective-permute-done.12 = f32[1024,128]{1,0:T(8,128)S(1)} collective-permute-done((f32[1024,128]{1,0:T(8,128)}, f32[1024,128]{1,0:T(8,128)S(1)}, u32[]{:S(2)}, u32[]{:S(2)}) %collective-permute-start.12) | collective-permute-done | bytes 524320 | tf_op jit(solution)/shard_map/ppermute | solution.py:23
  480.9 12.5 %collective-permute-done.13 = f32[1024,128]{1,0:T(8,128)S(1)} collective-permute-done((f32[1024,128]{1,0:T(8,128)S(1)}, f32[1024,128]{1,0:T(8,128)S(1)}, u32[]{:S(2)}, u32[]{:S(2)}) %collective-permute-start.13) | collective-permute-done | bytes 524320 | tf_op jit(solution)/shard_map/ppermute | solution.py:23
  493.7 11.6 %collective-permute-done.14 = f32[1024,128]{1,0:T(8,128)S(1)} collective-permute-done((f32[1024,128]{1,0:T(8,128)S(1)}, f32[1024,128]{1,0:T(8,128)S(1)}, u32[]{:S(2)}, u32[]{:S(2)}) %collective-permute-start.14) | collective-permute-done | bytes 524320 | tf_op jit(solution)/shard_map/ppermute | solution.py:23
  537.8 11.0 %collective-permute-done.15 = f32[1024,128]{1,0:T(8,128)S(1)} collective-permute-done((f32[1024,128]{1,0:T(8,128)}, f32[1024,128]{1,0:T(8,128)S(1)}, u32[]{:S(2)}, u32[]{:S(2)}) %collective-permute-start.15) | collective-permute-done | bytes 524320 | tf_op jit(solution)/shard_map/ppermute | solution.py:23
  548.8 10.5 %collective-permute-done.16 = f32[1024,128]{1,0:T(8,128)S(1)} collective-permute-done((f32[1024,128]{1,0:T(8,128)S(1)}, f32[1024,128]{1,0:T(8,128)S(1)}, u32[]{:S(2)}, u32[]{:S(2)}) %collective-permute-start.16) | collective-permute-done | bytes 524320 | tf_op jit(solution)/shard_map/ppermute | solution.py:23
  559.4 10.3 %collective-permute-done.17 = f32[1024,128]{1,0:T(8,128)S(1)} collective-permute-done((f32[1024,128]{1,0:T(8,128)S(1)}, f32[1024,128]{1,0:T(8,128)S(1)}, u32[]{:S(2)}, u32[]{:S(2)}) %collective-permute-start.17) | collective-permute-done | bytes 524320 | tf_op jit(solution)/shard_map/ppermute | solution.py:23
  602.7 141.8 %all-reduce.6.cloned.1.call-done = f32[128,128]{0,1:T(8,128)} async-done(((f32[128,128]{0,1:T(8,128)}), f32[128,128]{0,1:T(8,128)}) %all-reduce.6.cloned.1.call-update) | async-done | bytes 65552 | tf_op jit(solution)/shard_map/psum | solution.py:90
  746.4 11.7 %cholesky.55 = f32[128,128]{1,0:T(8,128)S(1)} custom-call(f32[128,128]{1,0:T(8,128)S(1)} %fusion.88), custom_call_target="Cholesky" | custom-call | tf_op jit(solution)/shard_map/jit(cholesky)/cholesky | solution.py:66
  774.0 12.5 %collective-permute-done.18 = f32[1024,128]{1,0:T(8,128)S(1)} collective-permute-done((f32[1024,128]{1,0:T(8,128)}, f32[1024,128]{1,0:T(8,128)S(1)}, u32[]{:S(2)}, u32[]{:S(2)}) %collective-permute-start.18) | collective-permute-done | bytes 524320 | tf_op jit(solution)/shard_map/ppermute | solution.py:23
  788.1 13.5 %collective-permute-done.19 = f32[1024,128]{1,0:T(8,128)S(1)} collective-permute-done((f32[1024,128]{1,0:T(8,128)S(1)}, f32[1024,128]{1,0:T(8,128)S(1)}, u32[]{:S(2)}, u32[]{:S(2)}) %collective-permute-start.19) | collective-permute-done | bytes 524320 | tf_op jit(solution)/shard_map/ppermute | solution.py:23
  801.8 14.2 %collective-permute-done.20 = f32[1024,128]{1,0:T(8,128)S(1)} collective-permute-done((f32[1024,128]{1,0:T(8,128)S(1)}, f32[1024,128]{1,0:T(8,128)S(1)}, u32[]{:S(2)}, u32[]{:S(2)}) %collective-permute-start.20) | collective-permute-done | bytes 524320 | tf_op jit(solution)/shard_map/ppermute | solution.py:23
  847.7 137.5 %all-reduce.8.cloned.1.call-done = f32[128,128]{0,1:T(8,128)} async-done(((f32[128,128]{0,1:T(8,128)}), f32[128,128]{0,1:T(8,128)}) %all-reduce.8.cloned.1.call-update) | async-done | bytes 65552 | tf_op jit(solution)/shard_map/psum | solution.py:94
  (170 shorter events, 294.4 us)
Async XLA Ops:
  7.2 68.7 %all-gather.8.cloned.1.call-start = ((), (), s32[]{:S(2)}) async-start(), calls=%async_computation | async-start | bytes 2162688 | tf_op jit(solution)/shard_map/all_gather | solution.py:33
  9.7 131.6 %all-gather.10.cloned.1.call-start = ((), (), s32[]{:S(2)}) async-start(), calls=%async_computation.1 | async-start | bytes 2162688 | tf_op jit(solution)/shard_map/all_gather | solution.py:33
  9.8 16.5 %collective-permute-start = (f32[1024,128]{1,0:T(8,128)}, f32[1024,128]{1,0:T(8,128)S(1)}, u32[]{:S(2)}, u32[]{:S(2)}) collective-permute-start(f32[1024,128]{1,0:T(8,128)} %param.13), channel_id=1, source_target_pairs={{0,1},{1,2},{2,3},{3,0},{4,5},{5,6},{6,7},{7,4},{8,9},{9,10},{10,1... | collective-permute-start | bytes 1572872 | tf_op jit(solution)/shard_map/ppermute | solution.py:23
  27.0 13.5 %collective-permute-start.1 = (f32[1024,128]{1,0:T(8,128)S(1)}, f32[1024,128]{1,0:T(8,128)}, u32[]{:S(2)}, u32[]{:S(2)}) collective-permute-start(f32[1024,128]{1,0:T(8,128)S(1)} %collective-permute-done), channel_id=1, source_target_pairs={{0,1},{1,2},{2,3},{3,0},{4,5},{5,6},{6,7},{7,4},{8,9},{9,10},{10,1... | collective-permute-start | bytes 1572872 | tf_op jit(solution)/shard_map/ppermute | solution.py:23
  40.6 12.9 %collective-permute-start.2 = (f32[1024,128]{1,0:T(8,128)}, f32[1024,128]{1,0:T(8,128)}, u32[]{:S(2)}, u32[]{:S(2)}) collective-permute-start(f32[1024,128]{1,0:T(8,128)} %collective-permute-done.1), channel_id=1, source_target_pairs={{0,1},{1,2},{2,3},{3,0},{4,5},{5,6},{6,7},{7,4},{8,9},{9,10},{10,1... | collective-permute-start | bytes 1572872 | tf_op jit(solution)/shard_map/ppermute | solution.py:23
  84.3 123.3 %all-gather.12.cloned.1.call-start = ((), (), s32[]{:S(2)}) async-start(), calls=%async_computation.2 | async-start | bytes 2162688 | tf_op jit(solution)/shard_map/all_gather | solution.py:33
  84.4 12.0 %collective-permute-start.3 = (f32[1024,128]{1,0:T(8,128)}, f32[1024,128]{1,0:T(8,128)S(1)}, u32[]{:S(2)}, u32[]{:S(2)}) collective-permute-start(f32[1024,128]{1,0:T(8,128)} %copy-done.9), channel_id=1, source_target_pairs={{0,1},{1,2},{2,3},{3,0},{4,5},{5,6},{6,7},{7,4},{8,9},{9,10},{10,1... | collective-permute-start | bytes 1572872 | tf_op jit(solution)/shard_map/ppermute | solution.py:23
  149.9 213.8 %all-reduce.4.cloned.1.call-start = ((), (), s32[]{:S(2)}) async-start(), calls=%async_computation.3 | async-start | bytes 131072 | tf_op jit(solution)/shard_map/psum | solution.py:90
  171.4 12.5 %collective-permute-start.8 = (f32[1024,128]{1,0:T(8,128)S(1)}, f32[1024,128]{1,0:T(8,128)S(1)}, u32[]{:S(2)}, u32[]{:S(2)}) collective-permute-start(f32[1024,128]{1,0:T(8,128)S(1)} %collective-permute-done.7), channel_id=1, source_target_pairs={{0,1},{1,2},{2,3},{3,0},{4,5},{5,6},{6,7},{7,4},{8,9},{9,10},{10,1... | collective-permute-start | bytes 1572872 | tf_op jit(solution)/shard_map/ppermute | solution.py:23
  216.6 242.1 %all-gather.14.cloned.1.call-start = ((), (), s32[]{:S(2)}) async-start(), calls=%async_computation.4 | async-start | bytes 2162688 | tf_op jit(solution)/shard_map/all_gather | solution.py:33
  391.8 137.2 %all-gather.16.cloned.1.call-start = ((), (), s32[]{:S(2)}) async-start(), calls=%async_computation.5 | async-start | bytes 2162688 | tf_op jit(solution)/shard_map/all_gather | solution.py:33
  391.9 13.7 %collective-permute-start.9 = (f32[1024,128]{1,0:T(8,128)}, f32[1024,128]{1,0:T(8,128)S(1)}, u32[]{:S(2)}, u32[]{:S(2)}) collective-permute-start(f32[1024,128]{1,0:T(8,128)} %copy-done.1), channel_id=1, source_target_pairs={{0,1},{1,2},{2,3},{3,0},{4,5},{5,6},{6,7},{7,4},{8,9},{9,10},{10,1... | collective-permute-start | bytes 1572872 | tf_op jit(solution)/shard_map/ppermute | solution.py:23
  405.6 15.1 %collective-permute-start.10 = (f32[1024,128]{1,0:T(8,128)S(1)}, f32[1024,128]{1,0:T(8,128)S(1)}, u32[]{:S(2)}, u32[]{:S(2)}) collective-permute-start(f32[1024,128]{1,0:T(8,128)S(1)} %collective-permute-done.9), channel_id=1, source_target_pairs={{0,1},{1,2},{2,3},{3,0},{4,5},{5,6},{6,7},{7,4},{8,9},{9,10},{10,1... | collective-permute-start | bytes 1572872 | tf_op jit(solution)/shard_map/ppermute | solution.py:23
  420.7 14.4 %collective-permute-start.11 = (f32[1024,128]{1,0:T(8,128)S(1)}, f32[1024,128]{1,0:T(8,128)S(1)}, u32[]{:S(2)}, u32[]{:S(2)}) collective-permute-start(f32[1024,128]{1,0:T(8,128)S(1)} %collective-permute-done.10), channel_id=1, source_target_pairs={{0,1},{1,2},{2,3},{3,0},{4,5},{5,6},{6,7},{7,4},{8,9},{9,10},{10,1... | collective-permute-start | bytes 1572872 | tf_op jit(solution)/shard_map/ppermute | solution.py:23
  467.2 126.3 %all-gather.18.cloned.1.call-start = ((), (), s32[]{:S(2)}) async-start(), calls=%async_computation.6 | async-start | bytes 2162688 | tf_op jit(solution)/shard_map/all_gather | solution.py:33
  467.2 13.6 %collective-permute-start.12 = (f32[1024,128]{1,0:T(8,128)}, f32[1024,128]{1,0:T(8,128)S(1)}, u32[]{:S(2)}, u32[]{:S(2)}) collective-permute-start(f32[1024,128]{1,0:T(8,128)} %copy-done.10), channel_id=1, source_target_pairs={{0,1},{1,2},{2,3},{3,0},{4,5},{5,6},{6,7},{7,4},{8,9},{9,10},{10,1... | collective-permute-start | bytes 1572872 | tf_op jit(solution)/shard_map/ppermute | solution.py:23
  480.9 12.5 %collective-permute-start.13 = (f32[1024,128]{1,0:T(8,128)S(1)}, f32[1024,128]{1,0:T(8,128)S(1)}, u32[]{:S(2)}, u32[]{:S(2)}) collective-permute-start(f32[1024,128]{1,0:T(8,128)S(1)} %collective-permute-done.12), channel_id=1, source_target_pairs={{0,1},{1,2},{2,3},{3,0},{4,5},{5,6},{6,7},{7,4},{8,9},{9,10},{10,1... | collective-permute-start | bytes 1572872 | tf_op jit(solution)/shard_map/ppermute | solution.py:23
  493.3 12.0 %collective-permute-start.14 = (f32[1024,128]{1,0:T(8,128)S(1)}, f32[1024,128]{1,0:T(8,128)S(1)}, u32[]{:S(2)}, u32[]{:S(2)}) collective-permute-start(f32[1024,128]{1,0:T(8,128)S(1)} %collective-permute-done.13), channel_id=1, source_target_pairs={{0,1},{1,2},{2,3},{3,0},{4,5},{5,6},{6,7},{7,4},{8,9},{9,10},{10,1... | collective-permute-start | bytes 1572872 | tf_op jit(solution)/shard_map/ppermute | solution.py:23
  537.7 206.9 %all-reduce.6.cloned.1.call-start = ((), (), s32[]{:S(2)}) async-start(), calls=%async_computation.7 | async-start | bytes 131072 | tf_op jit(solution)/shard_map/psum | solution.py:90
  602.5 237.2 %all-gather.20.cloned.1.call-start = ((), (), s32[]{:S(2)}) async-start(), calls=%async_computation.8 | async-start | bytes 2162688 | tf_op jit(solution)/shard_map/all_gather | solution.py:33
  772.7 212.4 %all-reduce.8.cloned.1.call-start = ((), (), s32[]{:S(2)}) async-start(), calls=%async_computation.9 | async-start | bytes 131072 | tf_op jit(solution)/shard_map/psum | solution.py:94
  772.8 13.7 %collective-permute-start.18 = (f32[1024,128]{1,0:T(8,128)}, f32[1024,128]{1,0:T(8,128)S(1)}, u32[]{:S(2)}, u32[]{:S(2)}) collective-permute-start(f32[1024,128]{1,0:T(8,128)} %copy-done.2), channel_id=1, source_target_pairs={{0,1},{1,2},{2,3},{3,0},{4,5},{5,6},{6,7},{7,4},{8,9},{9,10},{10,1... | collective-permute-start | bytes 1572872 | tf_op jit(solution)/shard_map/ppermute | solution.py:23
  786.5 15.1 %collective-permute-start.19 = (f32[1024,128]{1,0:T(8,128)S(1)}, f32[1024,128]{1,0:T(8,128)S(1)}, u32[]{:S(2)}, u32[]{:S(2)}) collective-permute-start(f32[1024,128]{1,0:T(8,128)S(1)} %collective-permute-done.18), channel_id=1, source_target_pairs={{0,1},{1,2},{2,3},{3,0},{4,5},{5,6},{6,7},{7,4},{8,9},{9,10},{10,1... | collective-permute-start | bytes 1572872 | tf_op jit(solution)/shard_map/ppermute | solution.py:23
  801.5 14.4 %collective-permute-start.20 = (f32[1024,128]{1,0:T(8,128)S(1)}, f32[1024,128]{1,0:T(8,128)S(1)}, u32[]{:S(2)}, u32[]{:S(2)}) collective-permute-start(f32[1024,128]{1,0:T(8,128)S(1)} %collective-permute-done.19), channel_id=1, source_target_pairs={{0,1},{1,2},{2,3},{3,0},{4,5},{5,6},{6,7},{7,4},{8,9},{9,10},{10,1... | collective-permute-start | bytes 1572872 | tf_op jit(solution)/shard_map/ppermute | solution.py:23
  (21 other events, 140.8 us)
Sparse Core Ops, SparseCore 0:
  10.8 47.0 all-gather.7
  84.4 45.0 all-gather.9
  150.0 47.8 all-gather.11
  216.8 146.8 all-reduce.3
  391.9 40.6 all-gather.13
  467.3 41.3 all-gather.15
  537.8 43.1 all-gather.17
  602.6 141.9 all-reduce.5
  772.8 40.6 all-gather.19
  847.8 137.3 all-reduce.7
